TPU v7x, 32 devices: a whole 2x2x4 slice. The times are simulated.
32 devices in a mesh: pipe: 2 (over core), ctx: 16 (over z, y, x).
Axes of the slice: x: 2, y: 2, z: 4, core: 2. Of those that a mesh axis runs over, the one named last changes fastest.
Arguments:
- arriving: bfloat16 [2, 4096, 2048], P('pipe', None, 'ctx'), may hold values from -6 to 6
- input_gate: bfloat16 [2, 4096, 2048], P('pipe', None, 'ctx'), may hold values from -6 to 6
- input_inner: bfloat16 [2, 4096, 2048], P('pipe', None, 'ctx'), may hold values from -6 to 6
- values: bfloat16 [2, 4096, 2048], P('pipe', None, 'ctx'), may hold values from -6 to 6
- conv_out: bfloat16 [2, 4096, 2048], P('pipe', None, 'ctx'), may hold values from -6 to 6
- filters: bfloat16 [2, 4096, 2048], P('pipe', None, 'ctx'), may hold values from -1 to 1
- bias: float32 [2, 4096], P('pipe'), may hold values from 0.5 to 1.5
Outputs:
- d_gate: bfloat16 [2, 4096, 2048], P('pipe', None, 'ctx')
- inner_gradient: bfloat16 [2, 4096, 2048], P('pipe', None, 'ctx')
- d_values: bfloat16 [2, 4096, 2048], P('pipe', None, 'ctx')
- d_filters: float32 [2, 4096, 2048], P('pipe', None, 'ctx')
All inputs are finite; a program needn't handle non-finite values.
Results may differ from a plain program's by a relative error of at most 0.011.
Values may be sent and summed in bfloat16 or wider, within the bound.
A program may use at most 128 MiB of HBM per device.

v0:
```python
import math

import jax
import jax.numpy as jnp
from jax import lax
from jax.sharding import PartitionSpec as P


def shifted(block, axis, distance):
    devices = range(lax.axis_size(axis))
    route = [((i - distance) % len(devices), i) for i in devices]
    return lax.ppermute(block, axis, route)


def angle_table(rows, cols, period, row_start, col_start):
    left = (jnp.arange(rows, dtype=jnp.int32) + row_start)[:, None]
    right = (jnp.arange(cols, dtype=jnp.int32) + col_start)[None, :]
    phase = (left * right % period).astype(jnp.float32) * (2.0 * math.pi / period)
    return (jnp.cos(phase), jnp.sin(phase))


def section_backward(other, gate_in, inner_in, values, saved, taps, bias, tables):
    cos_a, sin_a, cos_b, sin_b, cos_w, sin_w, cos_v, sin_v = tables
    tiles_list = cos_a.shape[0]
    channel_count, tokens_dev = values.shape
    per_peer = tokens_dev // tiles_list
    seq_length = tiles_list * tokens_dev
    lane_width = math.gcd(channel_count, 128)
    lane_groups = channel_count // lane_width
    grad = shifted(other, "pipe", -1)
    inner = (inner_in.astype(jnp.float32) * values.astype(jnp.float32)).astype(jnp.bfloat16)
    d_out = (grad.astype(jnp.float32) * gate_in.astype(jnp.float32)).astype(jnp.bfloat16)
    d_gate = (grad.astype(jnp.float32) * saved.astype(jnp.float32)).astype(jnp.bfloat16)

    def channels_last(array):
        return array.T.reshape(tiles_list, per_peer, lane_groups, lane_width)

    inner_cols, tap_cols = (
        lax.all_to_all(channels_last(inner), "ctx", split_axis=0, concat_axis=0, tiled=True),
        lax.all_to_all(channels_last(taps), "ctx", split_axis=0, concat_axis=0, tiled=True),
    )
    grad_cols = lax.all_to_all(channels_last(d_out), "ctx", split_axis=0, concat_axis=0, tiled=True)
    twist_cos = cos_w.T[:, :, None, None]
    rotation_sine = sin_w.T[:, :, None, None]

    def segment_first(columns):
        real_sum = jnp.einsum("argb,ak->krgb", columns, cos_a, preferred_element_type=jnp.float32)
        imag_sum = -jnp.einsum("argb,ak->krgb", columns, sin_a, preferred_element_type=jnp.float32)
        part_real = real_sum * twist_cos + imag_sum * rotation_sine
        part_imag = imag_sum * twist_cos - real_sum * rotation_sine
        return jnp.stack([part_real, part_imag]).astype(jnp.bfloat16)

    def segment_second(piece):
        part_real = piece[0]
        part_imag = piece[1]
        spec_real = jnp.einsum(
            "kjgb,jm->kmgb", part_real, cos_b, preferred_element_type=jnp.float32
        ) + jnp.einsum("kjgb,jm->kmgb", part_imag, sin_b, preferred_element_type=jnp.float32)
        spec_imag = jnp.einsum(
            "kjgb,jm->kmgb", part_imag, cos_b, preferred_element_type=jnp.float32
        ) - jnp.einsum("kjgb,jm->kmgb", part_real, sin_b, preferred_element_type=jnp.float32)
        return jnp.stack([spec_real, spec_imag]).astype(jnp.bfloat16)

    def spectrum(columns):
        return segment_second(
            lax.all_to_all(segment_first(columns), "ctx", split_axis=1, concat_axis=2, tiled=True)
        )

    inner_spec = spectrum(inner_cols).astype(jnp.float32)
    tap_spec = spectrum(tap_cols).astype(jnp.float32)
    grad_spec = spectrum(grad_cols).astype(jnp.float32)
    shrink = 1.0 / math.sqrt(seq_length)
    z_real, latent_quadrature = (inner_spec[0] * shrink, inner_spec[1] * shrink)
    h_real, h_imag = (tap_spec[0], tap_spec[1])
    d_real, d_imag = (grad_spec[0], grad_spec[1])
    q_real = (
        h_real * d_real + h_imag * d_imag - (z_real * d_imag - latent_quadrature * d_real)
    ).astype(jnp.bfloat16)
    q_imag = (
        h_real * d_imag - h_imag * d_real + z_real * d_real + latent_quadrature * d_imag
    ).astype(jnp.bfloat16)
    even_real = jnp.einsum(
        "kmgb,jm->kjgb", q_real, cos_b, preferred_element_type=jnp.float32
    ) - jnp.einsum("kmgb,jm->kjgb", q_imag, sin_b, preferred_element_type=jnp.float32)
    even_imag = jnp.einsum(
        "kmgb,jm->kjgb", q_imag, cos_b, preferred_element_type=jnp.float32
    ) + jnp.einsum("kmgb,jm->kjgb", q_real, sin_b, preferred_element_type=jnp.float32)
    local_cos = cos_v.T[:, :, None, None]
    local_sin = sin_v.T[:, :, None, None]
    back_real = even_real * local_cos - even_imag * local_sin
    back_imag = even_real * local_sin + even_imag * local_cos
    backward_parts = jnp.stack([back_real, back_imag]).astype(jnp.bfloat16)
    scale = 1.0 / (2 * seq_length)
    piece = lax.all_to_all(backward_parts, "ctx", split_axis=2, concat_axis=1, tiled=True)
    part_real = piece[0]
    part_imag = piece[1]
    out_real = (
        jnp.einsum("krgb,ak->argb", part_real, cos_a, preferred_element_type=jnp.float32)
        - jnp.einsum("krgb,ak->argb", part_imag, sin_a, preferred_element_type=jnp.float32)
    ) * scale
    out_imag = (
        jnp.einsum("krgb,ak->argb", part_imag, cos_a, preferred_element_type=jnp.float32)
        + jnp.einsum("krgb,ak->argb", part_real, sin_a, preferred_element_type=jnp.float32)
    ) * scale
    inverse_parts = jnp.stack([out_real, out_imag])
    bias_lanes = bias.reshape(lane_groups, lane_width)[None, None, :, :]
    grad_inner_cols = inverse_parts[0] + bias_lanes * grad_cols.astype(jnp.float32)
    gradient_tap_columns = inverse_parts[1]
    gradient_inner_part, grad_taps = (
        lax.all_to_all(
            grad_inner_cols.astype(jnp.bfloat16), "ctx", split_axis=0, concat_axis=0, tiled=True
        ).astype(grad_inner_cols.dtype),
        lax.all_to_all(
            gradient_tap_columns.astype(jnp.bfloat16),
            "ctx",
            split_axis=0,
            concat_axis=0,
            tiled=True,
        ).astype(gradient_tap_columns.dtype),
    )
    gradient_inner_part = gradient_inner_part.reshape(tokens_dev, channel_count).T
    grad_taps = grad_taps.reshape(tokens_dev, channel_count).T
    inner_gradient = (gradient_inner_part * values.astype(jnp.float32)).astype(jnp.bfloat16)
    d_values = (gradient_inner_part * inner_in.astype(jnp.float32)).astype(jnp.bfloat16)
    return (d_gate, inner_gradient, d_values, grad_taps)


def per_device(arriving, input_gate, input_inner, values, conv_out, filters, bias):
    tiles_list = lax.axis_size("ctx")
    my_index = lax.axis_index("ctx")
    tokens_dev = values.shape[2]
    per_peer = tokens_dev // tiles_list
    full_length = 2 * tiles_list * tokens_dev
    cos_a, sin_a = angle_table(tiles_list, 2 * tiles_list, 2 * tiles_list, 0, 0)
    cos_b, sin_b = angle_table(tokens_dev, tokens_dev, tokens_dev, 0, 0)
    cos_w, sin_w = angle_table(per_peer, 2 * tiles_list, full_length, my_index * per_peer, 0)
    cos_v, sin_v = angle_table(tokens_dev, 2, full_length, 0, my_index * 2)
    tables = (
        cos_a.astype(jnp.bfloat16),
        sin_a.astype(jnp.bfloat16),
        cos_b.astype(jnp.bfloat16),
        sin_b.astype(jnp.bfloat16),
        cos_w,
        sin_w,
        cos_v,
        sin_v,
    )
    results = section_backward(
        arriving[0],
        input_gate[0],
        input_inner[0],
        values[0],
        conv_out[0],
        filters[0],
        bias[0],
        tables,
    )
    return (results[0][None], results[1][None], results[2][None], results[3][None])


def solution(mesh):
    in_specs = (
        P("pipe", None, "ctx"),
        P("pipe", None, "ctx"),
        P("pipe", None, "ctx"),
        P("pipe", None, "ctx"),
        P("pipe", None, "ctx"),
        P("pipe", None, "ctx"),
        P("pipe", None),
    )
    out_specs = (
        P("pipe", None, "ctx"),
        P("pipe", None, "ctx"),
        P("pipe", None, "ctx"),
        P("pipe", None, "ctx"),
    )
    return jax.shard_map(
        per_device, mesh=mesh, in_specs=in_specs, out_specs=out_specs, check_vma=False
    )
```

profile of v0, /device:TPU:8, one launch (start us, length us, event | category | flops | bytes accessed | tf_op | source)
XLA Modules:
  0.0 622.5 jit_solution(16497502778437702817)
XLA Ops:
  5.5 7.2 %all-to-all-start.4 = ((bf16[16,8,32,128]{3,2,1,0:T(8,128)(2,1)}), bf16[16,8,32,128]{3,2,1,0:T(8,128)(2,1)S(1)}, u32[]{:S(2)}, u32[]{:S(2)}) async-start(bf16[16,8,32,128]{3,2,1,0:T(8,128)(2,1)} %bitcast.269), calls=%async_computation.4 | async-start | bytes 2097152 | tf_op jit(solution)/shard_map/all_to_all | solution.py:39
  14.5 23.8 %all-to-all-done.4 = bf16[16,8,32,128]{3,2,1,0:T(8,128)(2,1)S(1)} async-done(((bf16[16,8,32,128]{3,2,1,0:T(8,128)(2,1)}), bf16[16,8,32,128]{3,2,1,0:T(8,128)(2,1)S(1)}, u32[]{:S(2)}, u32[]{:S(2)}) %all-to-all-start.4) | async-done | bytes 1048608 | tf_op jit(solution)/shard_map/all_to_all | solution.py:39
  38.3 4.7 all-to-all-start
  50.1 17.1 %all-to-all-done = bf16[16,8,32,128]{3,2,1,0:T(8,128)(2,1)S(1)} async-done(((bf16[16,8,32,128]{3,2,1,0:T(8,128)(2,1)}), bf16[16,8,32,128]{3,2,1,0:T(8,128)(2,1)S(1)}, u32[]{:S(2)}, u32[]{:S(2)}) %all-to-all-start) | async-done | bytes 1048608 | tf_op jit(solution)/shard_map/all_to_all | solution.py:40
  67.2 5.1 all-to-all-start.2
  83.9 12.3 %all-to-all-done.2 = bf16[16,8,32,128]{3,2,1,0:T(8,128)(2,1)S(1)} async-done(((bf16[16,8,32,128]{3,2,1,0:T(8,128)(2,1)}), bf16[16,8,32,128]{3,2,1,0:T(8,128)(2,1)S(1)}, u32[]{:S(2)}, u32[]{:S(2)}) %all-to-all-start.2) | async-done | bytes 1048608 | tf_op jit(solution)/shard_map/all_to_all | solution.py:42
  98.8 10.7 %fusion.13 = (bf16[1,32,8,32,128]{4,1,3,2,0:T(8,128)(2,1)S(1)}, bf16[1,32,8,32,128]{4,1,3,2,0:T(8,128)(2,1)}, bf16[1,32,8,32,128]{4,1,3,2,0:T(8,128)(2,1)}, bf16...) fusion(f32[32,8,32,128]{3,0,2,1:T(8,128)S(1)} %copy-done.8, ...), kind=kOutput, calls=%fused_computation.51 | convolution fusion | flops 61873664 | bytes 34605056 | tf_op jit(solution)/shard_map/argb,ak->krgb/dot_general | solution.py:47
  113.5 4.9 all-to-all-start.1
  124.7 82.1 %all-to-all-done.1 = bf16[2,32,8,32,128]{4,3,2,0,1:T(8,128)(2,1)} async-done(((bf16[2,32,8,32,128]{4,3,2,0,1:T(8,128)(2,1)}), bf16[2,32,8,32,128]{4,3,2,0,1:T(8,128)(2,1)}, u32[]{:S(2)}, u32[]{:S(2)}) %all-to-all-start.1) | async-done | bytes 4194336 | tf_op jit(solution)/shard_map/all_to_all | solution.py:66
  206.8 7.9 %all-to-all-start.3 = ((bf16[2,32,8,32,128]{4,3,2,0,1:T(8,128)(2,1)}), bf16[2,32,8,32,128]{4,3,2,0,1:T(8,128)(2,1)}, u32[]{:S(2)}, u32[]{:S(2)}) async-start(bf16[2,32,8,32,128]{4,3,2,0,1:T(8,128)(2,1)} %copy.75), calls=%async_computation.3 | async-start | bytes 8388608 | tf_op jit(solution)/shard_map/all_to_all | solution.py:66
  220.3 84.2 %all-to-all-done.3 = bf16[2,32,8,32,128]{4,3,2,0,1:T(8,128)(2,1)} async-done(((bf16[2,32,8,32,128]{4,3,2,0,1:T(8,128)(2,1)}), bf16[2,32,8,32,128]{4,3,2,0,1:T(8,128)(2,1)}, u32[]{:S(2)}, u32[]{:S(2)}) %all-to-all-start.3) | async-done | bytes 4194336 | tf_op jit(solution)/shard_map/all_to_all | solution.py:66
  304.5 7.9 %all-to-all-start.5 = ((bf16[2,32,8,32,128]{4,3,2,0,1:T(8,128)(2,1)}), bf16[2,32,8,32,128]{4,3,2,0,1:T(8,128)(2,1)}, u32[]{:S(2)}, u32[]{:S(2)}) async-start(bf16[2,32,8,32,128]{4,3,2,0,1:T(8,128)(2,1)} %copy.85), calls=%async_computation.5 | async-start | bytes 8388608 | tf_op jit(solution)/shard_map/all_to_all | solution.py:66
  312.6 3.8 copy.164
  316.4 5.3 copy.163
  333.9 68.2 %all-to-all-done.5 = bf16[2,32,8,32,128]{4,3,2,0,1:T(8,128)(2,1)} async-done(((bf16[2,32,8,32,128]{4,3,2,0,1:T(8,128)(2,1)}), bf16[2,32,8,32,128]{4,3,2,0,1:T(8,128)(2,1)}, u32[]{:S(2)}, u32[]{:S(2)}) %all-to-all-start.5) | async-done | bytes 4194336 | tf_op jit(solution)/shard_map/all_to_all | solution.py:66
  402.1 3.8 copy.162
  429.0 4.6 subtract_convert_fusion
  443.8 100.7 %all_to_all.85 = bf16[2,2,128,32,128]{4,3,1,0,2:T(8,128)(2,1)S(1)} all-to-all(bf16[2,2,128,32,128]{4,3,1,0,2:T(8,128)(2,1)S(1)} %copy.91), channel_id=1, replica_groups=mesh['pipe'=2,'ctx'=16] {'ctx'}, dimensions={2} | all-to-all | bytes 8388608 | tf_op jit(solution)/shard_map/all_to_all | solution.py:94
  544.5 5.8 copy.161
  550.2 4.7 fusion.213
  559.2 4.8 all-to-all-start.7
  567.4 21.4 %all-to-all-done.7 = bf16[16,8,32,128]{3,2,1,0:T(8,128)(2,1)S(1)} async-done(((bf16[16,8,32,128]{3,2,1,0:T(8,128)(2,1)}), bf16[16,8,32,128]{3,2,1,0:T(8,128)(2,1)S(1)}, u32[]{:S(2)}, u32[]{:S(2)}) %all-to-all-start.7) | async-done | bytes 1048608 | tf_op jit(solution)/shard_map/all_to_all | solution.py:110
  589.7 4.7 all-to-all-start.8
  603.4 15.1 %all-to-all-done.8 = bf16[16,8,32,128]{3,2,1,0:T(8,128)(2,1)S(1)} async-done(((bf16[16,8,32,128]{3,2,1,0:T(8,128)(2,1)}), bf16[16,8,32,128]{3,2,1,0:T(8,128)(2,1)S(1)}, u32[]{:S(2)}, u32[]{:S(2)}) %all-to-all-start.8) | async-done | bytes 1048608 | tf_op jit(solution)/shard_map/all_to_all | solution.py:113
  (109 shorter events, 110.4 us)
Async XLA Ops:
  2.1 3.4 copy-start.15
  4.0 8.8 %copy-start.23 = (bf16[1,4096,128]{2,1,0:T(8,128)(2,1)S(1)}, bf16[1,4096,128]{2,1,0:T(8,128)(2,1)}, u32[]{:S(2)}) copy-start(bf16[1,4096,128]{2,1,0:T(8,128)(2,1)} %param.12) | copy-start | bytes 3145732
  5.5 32.8 %all-to-all-start.4 = ((bf16[16,8,32,128]{3,2,1,0:T(8,128)(2,1)}), bf16[16,8,32,128]{3,2,1,0:T(8,128)(2,1)S(1)}, u32[]{:S(2)}, u32[]{:S(2)}) async-start(bf16[16,8,32,128]{3,2,1,0:T(8,128)(2,1)} %bitcast.269), calls=%async_computation.4 | async-start | bytes 2097152 | tf_op jit(solution)/shard_map/all_to_all | solution.py:39
  12.8 30.3 %collective-permute-start = (bf16[4096,128]{1,0:T(8,128)(2,1)}, bf16[4096,128]{1,0:T(8,128)(2,1)}, u32[]{:S(2)}, u32[]{:S(2)}) collective-permute-start(bf16[4096,128]{1,0:T(8,128)(2,1)} %bitcast.295), channel_id=1, source_target_pairs={{16,0},{0,16},{17,1},{1,17},{18,2},{2,18},{19,3},{3,19},{20,4},{4,... | collective-permute-start | bytes 3145736 | tf_op jit(solution)/shard_map/ppermute | solution.py:12
  38.3 28.9 %all-to-all-start = ((bf16[16,8,32,128]{3,2,1,0:T(8,128)(2,1)}), bf16[16,8,32,128]{3,2,1,0:T(8,128)(2,1)S(1)}, u32[]{:S(2)}, u32[]{:S(2)}) async-start(bf16[16,8,32,128]{3,2,1,0:T(8,128)(2,1)} %bitcast.271), calls=%async_computation | async-start | bytes 2097152 | tf_op jit(solution)/shard_map/all_to_all | solution.py:40
  67.2 29.1 %all-to-all-start.2 = ((bf16[16,8,32,128]{3,2,1,0:T(8,128)(2,1)}), bf16[16,8,32,128]{3,2,1,0:T(8,128)(2,1)S(1)}, u32[]{:S(2)}, u32[]{:S(2)}) async-start(bf16[16,8,32,128]{3,2,1,0:T(8,128)(2,1)} %copy.167), calls=%async_computation.2 | async-start | bytes 2097152 | tf_op jit(solution)/shard_map/all_to_all | solution.py:42
  96.2 13.2 %copy-start.9 = (bf16[16,8,32,128]{3,2,1,0:T(8,128)(2,1)}, bf16[16,8,32,128]{3,2,1,0:T(8,128)(2,1)S(1)}, u32[]{:S(2)}) copy-start(bf16[16,8,32,128]{3,2,1,0:T(8,128)(2,1)S(1)} %all-to-all-done.2) | copy-start | bytes 3145732
  96.2 2.6 copy-start.8
  113.5 93.3 %all-to-all-start.1 = ((bf16[2,32,8,32,128]{4,3,2,0,1:T(8,128)(2,1)}), bf16[2,32,8,32,128]{4,3,2,0,1:T(8,128)(2,1)}, u32[]{:S(2)}, u32[]{:S(2)}) async-start(bf16[2,32,8,32,128]{4,3,2,0,1:T(8,128)(2,1)} %copy.66), calls=%async_computation.1 | async-start | bytes 8388608 | tf_op jit(solution)/shard_map/all_to_all | solution.py:66
  206.8 97.8 %all-to-all-start.3 = ((bf16[2,32,8,32,128]{4,3,2,0,1:T(8,128)(2,1)}), bf16[2,32,8,32,128]{4,3,2,0,1:T(8,128)(2,1)}, u32[]{:S(2)}, u32[]{:S(2)}) async-start(bf16[2,32,8,32,128]{4,3,2,0,1:T(8,128)(2,1)} %copy.75), calls=%async_computation.3 | async-start | bytes 8388608 | tf_op jit(solution)/shard_map/all_to_all | solution.py:66
  304.5 97.6 %all-to-all-start.5 = ((bf16[2,32,8,32,128]{4,3,2,0,1:T(8,128)(2,1)}), bf16[2,32,8,32,128]{4,3,2,0,1:T(8,128)(2,1)}, u32[]{:S(2)}, u32[]{:S(2)}) async-start(bf16[2,32,8,32,128]{4,3,2,0,1:T(8,128)(2,1)} %copy.85), calls=%async_computation.5 | async-start | bytes 8388608 | tf_op jit(solution)/shard_map/all_to_all | solution.py:66
  316.4 8.6 %copy-start.2 = (bf16[2,16,2,8,32,128]{5,3,1,4,2,0:T(8,128)(2,1)}, bf16[2,16,2,8,32,128]{5,3,1,4,2,0:T(8,128)(2,1)S(1)}, u32[]{:S(2)}) copy-start(bf16[2,16,2,8,32,128]{5,3,1,4,2,0:T(8,128)(2,1)S(1)} %copy.164) | copy-start | bytes 12582916
  321.7 9.3 %copy-start = (bf16[2,16,2,8,32,128]{5,3,1,4,2,0:T(8,128)(2,1)}, bf16[2,16,2,8,32,128]{5,3,1,4,2,0:T(8,128)(2,1)S(1)}, u32[]{:S(2)}) copy-start(bf16[2,16,2,8,32,128]{5,3,1,4,2,0:T(8,128)(2,1)S(1)} %copy.163) | copy-start | bytes 12582916
  406.9 2.7 copy-start.3
  409.7 2.8 copy-start.13
  412.5 4.2 copy-start.12
  416.7 2.8 copy-start.11
  423.8 2.8 copy-start.21
  433.6 2.7 copy-start.4
  554.9 3.1 copy-start.6
  559.2 29.5 %all-to-all-start.7 = ((bf16[16,8,32,128]{3,2,1,0:T(8,128)(2,1)}), bf16[16,8,32,128]{3,2,1,0:T(8,128)(2,1)S(1)}, u32[]{:S(2)}, u32[]{:S(2)}) async-start(bf16[16,8,32,128]{3,2,1,0:T(8,128)(2,1)} %copy.94), calls=%async_computation.7 | async-start | bytes 2097152 | tf_op jit(solution)/shard_map/all_to_all | solution.py:110
  566.1 29.9 %copy-start.16 = (bf16[1,4096,128]{1,2,0:T(8,128)(2,1)S(1)}, bf16[1,4096,128]{1,2,0:T(8,128)(2,1)}, u32[]{:S(2)}) copy-start(bf16[1,4096,128]{1,2,0:T(8,128)(2,1)} %copy-done.15) | copy-start | bytes 3145732
  566.1 29.9 %copy-start.18 = (bf16[1,4096,128]{1,2,0:T(8,128)(2,1)S(1)}, bf16[1,4096,128]{1,2,0:T(8,128)(2,1)}, u32[]{:S(2)}) copy-start(bf16[1,4096,128]{1,2,0:T(8,128)(2,1)} %copy-done.17) | copy-start | bytes 3145732
  589.7 28.8 %all-to-all-start.8 = ((bf16[16,8,32,128]{3,2,1,0:T(8,128)(2,1)}), bf16[16,8,32,128]{3,2,1,0:T(8,128)(2,1)S(1)}, u32[]{:S(2)}, u32[]{:S(2)}) async-start(bf16[16,8,32,128]{3,2,1,0:T(8,128)(2,1)} %copy.95), calls=%async_computation.8 | async-start | bytes 2097152 | tf_op jit(solution)/shard_map/all_to_all | solution.py:113
  (10 other events, 18.2 us)
where the time goes:
time: 627 us; the launch traced here: 623 us
  waiting for transfers between devices  324 us (52%)
  blocking collectives  101 us (16%)
  local copies, waits for them, and re-layouts  70.1 us (11%)
  matrix products  57.5 us (9%)
  starting transfers between devices  47.3 us (8%)
  other arithmetic  21.4 us (3%)
    all_to_all x3, waiting for transfers between devices, spectrum(): lax.all_to_all(segment_first(columns), 'ctx', split_axis=1, concat_axis=2...  235 us
    all_to_all x1, blocking collectives, section_backward(): lax.all_to_all(backward_parts, 'ctx', split_axis=2, concat_axis=1, tiled=...  101 us
    unnamed x59, local copies, waits for them, and re-layouts  28.8 us
    all_to_all x1, waiting for transfers between devices, section_backward(): lax.all_to_all(channels_last(inner), 'ctx', split_axis=0, concat_axis=0,...  23.8 us
    all_to_all x1, waiting for transfers between devices, section_backward(): lax.all_to_all(grad_inner_cols.astype(jnp.bfloat16), 'ctx', split_axis=0,...  21.4 us
    all_to_all x3, starting transfers between devices, spectrum(): lax.all_to_all(segment_first(columns), 'ctx', split_axis=1, concat_axis=2...  20.7 us
    all_to_all x1, waiting for transfers between devices, section_backward(): lax.all_to_all(channels_last(taps), 'ctx', split_axis=0, concat_axis=0, t...  17.1 us
    dot_general x3, matrix products, segment_first(): jnp.einsum('argb,ak->krgb', columns, cos_a, preferred_element_type=jnp.fl...  16.4 us
  transfers between devices with their start and end apart: 9, of which 8 were waited for; matrix products, arithmetic and copies ran while one was open for 10% of the time, Pallas kernels for 0%

commit v1 on v0

v1 whole, which is shorter than its diff:
```python
import functools
import math

import jax
import jax.numpy as jnp
import numpy as np
from jax import lax
from jax.experimental import pallas as pl
from jax.experimental.pallas import tpu as pltpu
from jax.sharding import PartitionSpec as P


def plus(a, b):
    return b if a is None else a if b is None else a + b


def minus(a, b):
    return a if b is None else -b if a is None else a - b


def turn(a, b, k, n):
    k = k % n
    if k == 0:
        return a, b
    if 4 * k == n:
        return b, minus(None, a)
    if 4 * k == 3 * n:
        return minus(None, b), a
    c, s = math.cos(2 * math.pi * k / n), math.sin(2 * math.pi * k / n)

    def scaled(v, f):
        return None if v is None else v * f

    if 8 * k == n:
        return scaled(plus(a, b), c), scaled(minus(b, a), c)
    return plus(scaled(a, c), scaled(b, s)), minus(scaled(b, c), scaled(a, s))


def real_dft(x, n):
    if n == 2:
        return [(x[0], None), (x[0], None)]
    even, odd = real_dft(x[0::2], n // 2), real_dft(x[1::2], n // 2)
    out = [None] * (n // 2 + 1)
    for k in range(n // 4 + 1):
        er, ei = even[k]
        tr, ti = turn(*odd[k], k, n)
        if 4 * k == n:
            out[k] = (plus(er, tr), plus(ei, ti))
        else:
            out[k] = (plus(er, tr), plus(ei, ti))
            out[n // 2 - k] = (minus(er, tr), minus(ti, ei))
    return out


def real_inverse(spec, n):
    if n == 2:
        return [plus(spec[0][0], spec[1][0])]
    even, odd = [], []
    for k in range(n // 4 + 1):
        xr, xi = spec[k]
        if 4 * k == n:
            even.append((xr + xr, None))
            odd.append((minus(None, None if xi is None else xi + xi), None))
            continue
        yr, yi = spec[n // 2 - k]
        even.append((plus(xr, yr), minus(xi, yi)))
        dr, di = minus(xr, yr), plus(xi, yi)
        odd.append(turn(dr, di, -k, n))
    even[0], odd[0] = (even[0][0], None), (odd[0][0], None)
    first, second = real_inverse(even, n // 2), real_inverse(odd, n // 2)
    return [v for pair in zip(first, second) for v in pair]


def tables(tiles, tokens):
    full = 2 * tiles * tokens
    j = np.arange(tokens)
    phase = 2 * np.pi * ((j[:, None] * j[None, :]) % tokens) / tokens
    cb, sb = np.cos(phase), np.sin(phase)
    forward = np.block([[cb, -sb], [sb, cb]])
    k = np.arange(tiles + 1)
    angle = 2 * np.pi * ((k[:, None] * j[None, :]) % full) / full
    twist = np.stack([np.cos(angle), np.sin(angle)], axis=1)
    return (
        jnp.asarray(forward, jnp.bfloat16),
        jnp.asarray(forward.T, jnp.bfloat16),
        jnp.asarray(twist, jnp.float32),
    )


ROWS = 16


def transform(rx, out, w, wi, twist, spec, back):
    _, tiles, rows, tokens = rx.shape
    full = 2 * tiles * tokens
    shrink = 1.0 / math.sqrt(tiles * tokens)
    steps = rows // ROWS

    def first(t, carry):
        s, i = t // steps, t % steps
        at = pl.ds(pl.multiple_of(i * ROWS, ROWS), ROWS)
        x = [rx[s, a, at, :].astype(jnp.float32) for a in range(tiles)]
        for k, (re, im) in enumerate(real_dft(x, 2 * tiles)):
            if k == 0:
                new_re, new_im = re, jnp.zeros_like(re)
            else:
                c, d = twist[k, 0:1, :], twist[k, 1:2, :]
                new_re = plus(re * c, None if im is None else im * d)
                new_im = minus(None if im is None else im * c, re * d)
            spec[s, k, at, 0:tokens] = new_re.astype(jnp.bfloat16)
            spec[s, k, at, tokens : 2 * tokens] = new_im.astype(jnp.bfloat16)
        return carry

    lax.fori_loop(0, 3 * steps, first, 0)

    def middle(k, carry):
        def spectrum(s):
            u = jnp.dot(spec[s, k], w[...], preferred_element_type=jnp.float32)
            u = u.astype(jnp.bfloat16).astype(jnp.float32)
            return u[:, :tokens], u[:, tokens:]

        hr, hi = spectrum(0)
        zr, zi = spectrum(1)
        dr, di = spectrum(2)
        c = twist[k, 0:1, :] * (1.0 / full)
        d = twist[k, 1:2, :] * (1.0 / full)
        for s, (ur, ui, f) in enumerate(((hr, hi, 1.0), (zr, zi, shrink))):
            qr = ur * dr + ui * di
            qi = ur * di - ui * dr
            if s:
                qr, qi = qr * f, qi * f
            q = jnp.concatenate([qr, qi], axis=1).astype(jnp.bfloat16)
            e = jnp.dot(q, wi[...], preferred_element_type=jnp.float32)
            er, ei = e[:, :tokens], e[:, tokens:]
            back[s, k, :, 0:tokens] = (er * c - ei * d).astype(jnp.bfloat16)
            back[s, k, :, tokens : 2 * tokens] = (er * d + ei * c).astype(jnp.bfloat16)
        return carry

    lax.fori_loop(0, tiles + 1, middle, 0)

    def last(t, carry):
        s, i = t // steps, t % steps
        at = pl.ds(pl.multiple_of(i * ROWS, ROWS), ROWS)
        pieces = []
        for k in range(tiles + 1):
            re = back[s, k, at, 0:tokens].astype(jnp.float32)
            im = None
            if 0 < k < tiles:
                im = back[s, k, at, tokens : 2 * tokens].astype(jnp.float32)
            pieces.append((re, im))
        for a, value in enumerate(real_inverse(pieces, 2 * tiles)):
            out[s, a, at, :] = value.astype(jnp.bfloat16)
        return carry

    lax.fori_loop(0, 2 * steps, last, 0)


def local_call(received):
    _, tiles, own, tokens = received.shape
    w, wi, twist = tables(tiles, tokens)

    def body(rx, w_ref, wi_ref, twist_ref, out, spec, back):
        transform(rx, out, w_ref, wi_ref, twist_ref, spec, back)

    group = max(ROWS, own // 4)

    def whole(shape):
        return pl.BlockSpec(shape, lambda g: (0,) * len(shape))

    return pl.pallas_call(
        body,
        grid=(own // group,),
        in_specs=[
            pl.BlockSpec((3, tiles, group, tokens), lambda g: (0, 0, g, 0)),
            whole(w.shape),
            whole(wi.shape),
            whole(twist.shape),
        ],
        out_specs=pl.BlockSpec((2, tiles, group, tokens), lambda g: (0, 0, g, 0)),
        out_shape=jax.ShapeDtypeStruct((2, tiles, own, tokens), jnp.bfloat16),
        scratch_shapes=[
            pltpu.VMEM((3, tiles + 1, group, 2 * tokens), jnp.bfloat16),
            pltpu.VMEM((2, tiles + 1, group, 2 * tokens), jnp.bfloat16),
        ],
        compiler_params=pltpu.CompilerParams(vmem_limit_bytes=56 * 2**20),
    )(received, w, wi, twist)


def per_device(arriving, input_gate, input_inner, values, conv_out, filters, bias):
    tiles = lax.axis_size("ctx")
    sections = lax.axis_size("pipe")
    channels, tokens = values.shape[1:]
    own = channels // tiles
    f32, bf16 = jnp.float32, jnp.bfloat16
    route = [((i + 1) % sections, i) for i in range(sections)]
    grad = lax.ppermute(arriving[0], "pipe", route).astype(f32)
    inner_in, vals = input_inner[0].astype(f32), values[0].astype(f32)
    inner = (inner_in * vals).astype(bf16)
    d_out = (grad * input_gate[0].astype(f32)).astype(bf16)
    d_gate = (grad * conv_out[0].astype(f32)).astype(bf16)
    sent = jnp.stack([filters[0], inner, d_out]).reshape(3, tiles, own, tokens)
    received = lax.all_to_all(sent, "ctx", split_axis=1, concat_axis=1, tiled=True)
    result = local_call(received)
    q = lax.all_to_all(result, "ctx", split_axis=1, concat_axis=1, tiled=True)
    q = q.reshape(2, channels, tokens).astype(f32)
    dz = q[0] + bias[0][:, None] * d_out.astype(f32)
    inner_gradient = (dz * vals).astype(bf16)
    d_values = (dz * inner_in).astype(bf16)
    return (d_gate[None], inner_gradient[None], d_values[None], q[1][None])


def solution(mesh):
    spread = P("pipe", None, "ctx")
    return jax.shard_map(
        per_device,
        mesh=mesh,
        in_specs=(spread,) * 6 + (P("pipe", None),),
        out_specs=(spread,) * 4,
        check_vma=False,
    )
```

time: 627 us -> 180 us (0.29)
  waiting for transfers between devices: 324 us -> 0.9 us
  local copies, waits for them, and re-layouts: 70.1 us -> 5.63 us
  matrix products: 57.5 us -> 0 us
  starting transfers between devices: 47.3 us -> 0.07 us
  Pallas kernels: 0 us -> 35 us
  blocking collectives: 101 us -> 130 us
  other arithmetic: 21.4 us -> 5.73 us
    all_to_all x8 -> x0, waiting for transfers between devices: 324 us -> none  [the longest x3 235 us: spectrum(): lax.all_to_all(segment_first(columns), 'ctx', split_axis=1, concat_axis=2...]
    dot_general x26 -> x0, matrix products: 57.5 us -> none  [the longest x3 16.4 us: segment_first(): jnp.einsum('argb,ak->krgb', columns, cos_a, preferred_element_type=jnp.fl...]
    all_to_all x8 -> x0, starting transfers between devices: 47.3 us -> none  [the longest x3 20.7 us: spectrum(): lax.all_to_all(segment_first(columns), 'ctx', split_axis=1, concat_axis=2...]
    pallas_call x0 -> x1, Pallas kernels: none -> 35 us  [local_call(): pl.pallas_call(body, grid=(own // group,), in_specs=[pl.BlockSpec((3, til...]
    all_to_all x1 -> x2, blocking collectives: 101 us -> 130 us  [the longest x1 78 us: per_device(): lax.all_to_all(sent, 'ctx', split_axis=1, concat_axis=1, tiled=True)]
    unnamed x59 -> x12, local copies, waits for them, and re-layouts: 28.8 us -> 0.03 us
    all_to_all x4 -> x1, local copies, waits for them, and re-layouts: 18.7 us -> 1.99 us  [per_device(): lax.all_to_all(sent, 'ctx', split_axis=1, concat_axis=1, tiled=True)]
    another operation x4 -> x0, local copies, waits for them, and re-layouts: 13.7 us -> none  [the longest x3 11 us: segment_first(): return jnp.stack([part_real, part_imag]).astype(jnp.bfloat16)]
  transfers between devices with their start and end apart: 9 -> 1, of which waited for: 8 -> 1; matrix products, arithmetic and copies ran while one was open for 10% -> 1% of each run, Pallas kernels for 0% -> 0%
where the time goes in v1:
time: 180 us; the launch traced here: 178 us
  blocking collectives  130 us (72%)
  Pallas kernels  35 us (19%)
  other arithmetic  5.73 us (3%)
  local copies, waits for them, and re-layouts  5.63 us (3%)
    all_to_all x1, blocking collectives, per_device(): lax.all_to_all(sent, 'ctx', split_axis=1, concat_axis=1, tiled=True)  78 us
    all_to_all x1, blocking collectives, per_device(): q = lax.all_to_all(result, 'ctx', split_axis=1, concat_axis=1, tiled=True)  51.9 us
    pallas_call x1, Pallas kernels, local_call(): pl.pallas_call(body, grid=(own // group,), in_specs=[pl.BlockSpec((3, til...  35 us
  transfers between devices with their start and end apart: 1, of which 1 were waited for; matrix products, arithmetic and copies ran while one was open for 1% of the time, Pallas kernels for 0%

profile of v1, /device:TPU:8, one launch (start us, length us, event | category | flops | bytes accessed | tf_op | source)
XLA Modules:
  0.0 177.9 jit_solution(12798317206179731122)
XLA Ops:
  0.6 0.0 copy-start.3
  0.6 0.0 copy-start.2
  0.7 0.1 collective-permute-start
  0.7 1.9 %fusion.4 = bf16[1,4096,128]{2,1,0:T(8,128)(2,1)S(1)} fusion(bf16[1,4096,128]{2,1,0:T(8,128)(2,1)} %param.13, bf16[1,4096,128]{2,1,0:T(8,128)(2,1)} %param.12), kind=kLoop, calls=%fused_computation.10 | loop fusion | flops 2097152 | bytes 3145728 | tf_op jit(solution)/shard_map/convert_element_type | solution.py:198
  2.7 0.0 copy-start.4
  2.7 0.9 collective-permute-done
  3.6 0.0 copy-done.3
  3.6 0.0 copy-done.2
  3.6 1.4 fusion.1
  5.0 0.0 copy-done.4
  5.0 0.3 pad_maximum_fusion
  5.4 78.0 %all_to_all.10 = bf16[3,16,256,128]{3,2,0,1:T(8,128)(2,1)S(1)} all-to-all(bf16[3,16,256,128]{3,2,0,1:T(8,128)(2,1)S(1)} %pad_maximum_fusion), channel_id=1, replica_groups=mesh['pipe'=2,'ctx'=16] {'ctx'}, dimensions={1} | all-to-all | bytes 6291456 | tf_op jit(solution)/shard_map/all_to_all | solution.py:202
  83.3 2.0 %copy.14.rx = bf16[3,16,256,128]{3,2,1,0:T(8,128)(2,1)} copy(bf16[3,16,256,128]{3,2,0,1:T(8,128)(2,1)S(1)} %all_to_all.10) | data formatting | bytes 6291456 | tf_op jit(solution)/shard_map/all_to_all | solution.py:202
  85.3 35.0 %shard_map.129 = bf16[2,16,256,128]{3,2,1,0:T(8,128)(2,1)} custom-call(bf16[3,16,256,128]{3,2,1,0:T(8,128)(2,1)} %copy.14.rx, bf16[256,256]{1,0:T(8,128)(2,1)} %constant.6.clone.w_ref, bf16[256,256]{1,0:T(8,128)(2,1)} %constant.7.clone.wi_ref, f32[17,2,128]{2,1,0:T(2,128)} %constant.8.clone.twist_ref), custom_call_target="tpu_custom_call" | custom-call | tf_op jit(solution)/shard_map/pallas_call | solution.py:170
  120.4 1.8 %copy.15 = bf16[2,16,256,128]{3,2,0,1:T(8,128)(2,1)S(1)} copy(bf16[2,16,256,128]{3,2,1,0:T(8,128)(2,1)} %shard_map.129) | data formatting | bytes 4194304 | tf_op jit(solution)/shard_map/pallas_call | solution.py:170
  122.2 51.9 %all_to_all.11 = bf16[2,16,256,128]{3,2,0,1:T(8,128)(2,1)S(1)} all-to-all(bf16[2,16,256,128]{3,2,0,1:T(8,128)(2,1)S(1)} %copy.15), channel_id=1, replica_groups=mesh['pipe'=2,'ctx'=16] {'ctx'}, dimensions={1} | all-to-all | bytes 4194304 | tf_op jit(solution)/shard_map/all_to_all | solution.py:204
  174.1 0.0 copy-start
  174.1 0.0 copy-start.1
  174.1 0.0 copy-start.5
  174.1 1.8 %fusion.8 = (f32[1,16,256,128]{3,2,0,1:T(8,128)}, f32[1,16,256,128]{3,2,0,1:T(8,128)S(1)}) fusion(bf16[2,16,256,128]{3,2,0,1:T(8,128)(2,1)S(1)} %all_to_all.11), kind=kLoop, calls=%fused_computation.15 | loop fusion | bytes 8388608 | tf_op jit(solution)/shard_map/slice | solution.py:209
  175.9 0.0 copy-done
  175.9 0.0 copy-done.1
  175.9 0.0 copy-done.5
  175.9 2.0 %fusion.3 = (bf16[4096,128]{1,0:T(8,128)(2,1)}, bf16[4096,128]{1,0:T(8,128)(2,1)}) fusion(bf16[1,4096,128]{2,1,0:T(8,128)(2,1)S(1)} %copy-done, bf16[4096,128]{1,0:T(8,128)(2,1)S(1)} %get-tuple-element.8, f32[1,16,256,128]{3,2,0,1:T(8,128)S(1)} %get-tuple-element.7, f32[4096]{0:T(1024)S(1)} %bitcast.40, bf16[1,4096,128]{2,1,0:T(8,128)(2,1)S(1)} %copy-done.1), kind=kLoop, calls=%fused_computation.9 | loop fusion | flops 4718592 | bytes 7356416 | tf_op jit(solution)/shard_map/convert_element_type | solution.py:208
Async XLA Ops:
  0.6 3.0 %copy-start.3 = (bf16[1,4096,128]{2,1,0:T(8,128)(2,1)S(1)}, bf16[1,4096,128]{2,1,0:T(8,128)(2,1)}, u32[]{:S(2)}) copy-start(bf16[1,4096,128]{2,1,0:T(8,128)(2,1)} %param.14) | copy-start | bytes 3145732
  0.6 3.0 %copy-start.2 = (bf16[1,4096,128]{2,1,0:T(8,128)(2,1)S(1)}, bf16[1,4096,128]{2,1,0:T(8,128)(2,1)}, u32[]{:S(2)}) copy-start(bf16[1,4096,128]{2,1,0:T(8,128)(2,1)} %param.11) | copy-start | bytes 3145732
  0.7 2.9 %collective-permute-start = (bf16[4096,128]{1,0:T(8,128)(2,1)}, bf16[4096,128]{1,0:T(8,128)(2,1)S(1)}, u32[]{:S(2)}, u32[]{:S(2)}) collective-permute-start(bf16[4096,128]{1,0:T(8,128)(2,1)} %bitcast.41), channel_id=1, source_target_pairs={{16,0},{0,16},{17,1},{1,17},{18,2},{2,18},{19,3},{3,19},{20,4},{4,... | collective-permute-start | bytes 3145736 | tf_op jit(solution)/shard_map/ppermute | solution.py:196
  2.7 2.4 %copy-start.4 = (bf16[1,4096,128]{2,1,0:T(8,128)(2,1)S(1)}, bf16[1,4096,128]{2,1,0:T(8,128)(2,1)}, u32[]{:S(2)}) copy-start(bf16[1,4096,128]{2,1,0:T(8,128)(2,1)} %param.15) | copy-start | bytes 3145732
  174.1 1.8 %copy-start = (bf16[1,4096,128]{2,1,0:T(8,128)(2,1)S(1)}, bf16[1,4096,128]{2,1,0:T(8,128)(2,1)}, u32[]{:S(2)}) copy-start(bf16[1,4096,128]{2,1,0:T(8,128)(2,1)} %param.12) | copy-start | bytes 3145732
  174.1 1.8 %copy-start.1 = (bf16[1,4096,128]{2,1,0:T(8,128)(2,1)S(1)}, bf16[1,4096,128]{2,1,0:T(8,128)(2,1)}, u32[]{:S(2)}) copy-start(bf16[1,4096,128]{2,1,0:T(8,128)(2,1)} %param.13) | copy-start | bytes 3145732
  174.1 1.8 %copy-start.5 = (f32[1,4096]{1,0:T(1,128)S(1)}, f32[1,4096]{1,0:T(1,128)}, u32[]{:S(2)}) copy-start(f32[1,4096]{1,0:T(1,128)} %param.16) | copy-start | bytes 49156

commit v2 on v1

--- a/solution.py
+++ b/solution.py
@@ -97,7 +97,7 @@
     steps = rows // ROWS
 
     def first(t, carry):
-        s, i = t // steps, t % steps
+        s, i = lax.div(t, steps), lax.rem(t, steps)
         at = pl.ds(pl.multiple_of(i * ROWS, ROWS), ROWS)
         x = [rx[s, a, at, :].astype(jnp.float32) for a in range(tiles)]
         for k, (re, im) in enumerate(real_dft(x, 2 * tiles)):
@@ -139,7 +139,7 @@
     lax.fori_loop(0, tiles + 1, middle, 0)
 
     def last(t, carry):
-        s, i = t // steps, t % steps
+        s, i = lax.div(t, steps), lax.rem(t, steps)
         at = pl.ds(pl.multiple_of(i * ROWS, ROWS), ROWS)
         pieces = []
         for k in range(tiles + 1):
@@ -155,35 +155,182 @@
     lax.fori_loop(0, 2 * steps, last, 0)
 
 
-def local_call(received):
-    _, tiles, own, tokens = received.shape
-    w, wi, twist = tables(tiles, tokens)
-
-    def body(rx, w_ref, wi_ref, twist_ref, out, spec, back):
-        transform(rx, out, w_ref, wi_ref, twist_ref, spec, back)
-
+MESH = pl.DeviceIdType.MESH
+
+
+def kernel(
+    n, sections, group,
+    arriving, taps, gate, inner_in, vals, w, wi, twist,
+    grad_out, q,
+    grad, stage, rx, res, spec, back,
+    pair_send, pair_recv, send, recv, home, back_send, back_recv, back_home, grad_home,
+):
+    me, sec = lax.axis_index("ctx"), lax.axis_index("pipe")
+    groups = arriving.shape[1] // group
+
+    def rows_of(g):
+        return pl.ds(pl.multiple_of(g * group, group), group)
+
+    def peer_of(d):
+        return lax.rem(me + d, n)
+
+    barrier = pltpu.get_barrier_semaphore()
+    pl.semaphore_signal(
+        barrier, inc=1, device_id={"pipe": lax.rem(sec + 1, sections)}, device_id_type=MESH
+    )
+
+    def greet(d, carry):
+        pl.semaphore_signal(barrier, inc=1, device_id={"ctx": peer_of(d)}, device_id_type=MESH)
+        return carry
+
+    lax.fori_loop(1, n, greet, 0)
+    pl.semaphore_wait(barrier, n)
+
+    def pair(g):
+        return pltpu.make_async_remote_copy(
+            src_ref=arriving.at[:, rows_of(g)],
+            dst_ref=grad.at[:, rows_of(g)],
+            send_sem=pair_send.at[g],
+            recv_sem=pair_recv.at[g],
+            device_id={"pipe": lax.rem(sec + sections - 1, sections)},
+            device_id_type=MESH,
+        )
+
+    def start_pair(g, carry):
+        pair(g).start()
+        return carry
+
+    lax.fori_loop(0, groups, start_pair, 0)
+
+    def ship(src, g, s, p):
+        pltpu.make_async_remote_copy(
+            src_ref=src,
+            dst_ref=rx.at[g, s, me],
+            send_sem=send.at[g],
+            recv_sem=recv.at[g],
+            device_id={"ctx": p},
+            device_id_type=MESH,
+        ).start()
+
+    def own_taps(g):
+        return pltpu.make_async_copy(taps.at[me, rows_of(g)], rx.at[g, 0, me], home.at[g])
+
+    def keep_grad(g):
+        return pltpu.make_async_copy(
+            grad.at[:, rows_of(g)], grad_out.at[:, rows_of(g)], grad_home.at[g]
+        )
+
+    def forward(g, carry):
+        rows = rows_of(g)
+
+        def send_taps(d, c):
+            ship(taps.at[peer_of(d), rows], g, 0, peer_of(d))
+            return c
+
+        lax.fori_loop(1, n, send_taps, 0)
+        own_taps(g).start()
+
+        def product(left, right, s):
+            def one(p):
+                return (left[p, rows].astype(jnp.float32) * right[p, rows].astype(jnp.float32)).astype(
+                    jnp.bfloat16
+                )
+
+            def make(d, c):
+                stage[g, s - 1, peer_of(d)] = one(peer_of(d))
+                return c
+
+            lax.fori_loop(1, n, make, 0)
+            rx[g, s, me] = one(me)
+
+            def post(d, c):
+                ship(stage.at[g, s - 1, peer_of(d)], g, s, peer_of(d))
+                return c
+
+            lax.fori_loop(1, n, post, 0)
+
+        product(inner_in, vals, 1)
+        pair(g).wait_recv()
+        keep_grad(g).start()
+        product(grad, gate, 2)
+        return carry
+
+    lax.fori_loop(0, groups, forward, 0)
+
+    def own_result(g):
+        return pltpu.make_async_copy(
+            res.at[g, :, me], q.at[:, me, rows_of(g)], back_home.at[g]
+        )
+
+    def turn_group(g, carry):
+        landed = rx.at[g, :, pl.ds(0, n - 1)]
+        pltpu.make_async_copy(landed, landed, recv.at[g]).wait()
+        own_taps(g).wait()
+        transform(rx.at[g], res.at[g], w, wi, twist, spec, back)
+
+        def reply(d, c):
+            pltpu.make_async_remote_copy(
+                src_ref=res.at[g, :, peer_of(d)],
+                dst_ref=q.at[:, me, rows_of(g)],
+                send_sem=back_send.at[g],
+                recv_sem=back_recv.at[0],
+                device_id={"ctx": peer_of(d)},
+                device_id_type=MESH,
+            ).start()
+            return c
+
+        lax.fori_loop(1, n, reply, 0)
+        own_result(g).start()
+        return carry
+
+    lax.fori_loop(0, groups, turn_group, 0)
+
+    def finish(g, carry):
+        pair(g).wait_send()
+        keep_grad(g).wait()
+        own_result(g).wait()
+        sent = rx.at[g, :, pl.ds(0, n - 1)]
+        pltpu.make_async_copy(sent, sent, send.at[g]).wait()
+        replied = res.at[g, :, pl.ds(0, n - 1)]
+        pltpu.make_async_copy(replied, replied, back_send.at[g]).wait()
+        return carry
+
+    lax.fori_loop(0, groups, finish, 0)
+    everything = q.at[:, pl.ds(0, n - 1)]
+    pltpu.make_async_copy(everything, everything, back_recv.at[0]).wait()
+
+
+def exchange(arriving, taps, gate, inner_in, vals, n, sections):
+    _, own, tokens = arriving.shape
     group = max(ROWS, own // 4)
-
-    def whole(shape):
-        return pl.BlockSpec(shape, lambda g: (0,) * len(shape))
-
+    groups = own // group
+    w, wi, twist = tables(n, tokens)
+    bf16 = jnp.bfloat16
+    vmem = pl.BlockSpec(memory_space=pltpu.VMEM)
+    hbm = pl.BlockSpec(memory_space=pl.ANY)
+    dma = pltpu.SemaphoreType.DMA
     return pl.pallas_call(
-        body,
-        grid=(own // group,),
-        in_specs=[
-            pl.BlockSpec((3, tiles, group, tokens), lambda g: (0, 0, g, 0)),
-            whole(w.shape),
-            whole(wi.shape),
-            whole(twist.shape),
+        functools.partial(kernel, n, sections, group),
+        in_specs=[hbm, hbm, vmem, vmem, vmem, vmem, vmem, vmem],
+        out_specs=[hbm, hbm],
+        out_shape=[
+            jax.ShapeDtypeStruct((n, own, tokens), bf16),
+            jax.ShapeDtypeStruct((2, n, own, tokens), bf16),
         ],
-        out_specs=pl.BlockSpec((2, tiles, group, tokens), lambda g: (0, 0, g, 0)),
-        out_shape=jax.ShapeDtypeStruct((2, tiles, own, tokens), jnp.bfloat16),
         scratch_shapes=[
-            pltpu.VMEM((3, tiles + 1, group, 2 * tokens), jnp.bfloat16),
-            pltpu.VMEM((2, tiles + 1, group, 2 * tokens), jnp.bfloat16),
+            pltpu.VMEM((n, own, tokens), bf16),
+            pltpu.VMEM((groups, 2, n, group, tokens), bf16),
+            pltpu.VMEM((groups, 3, n, group, tokens), bf16),
+            pltpu.VMEM((groups, 2, n, group, tokens), bf16),
+            pltpu.VMEM((3, n + 1, group, 2 * tokens), bf16),
+            pltpu.VMEM((2, n + 1, group, 2 * tokens), bf16),
+            dma((groups,)), dma((groups,)), dma((groups,)), dma((groups,)), dma((groups,)),
+            dma((groups,)), dma((1,)), dma((groups,)), dma((groups,)),
         ],
-        compiler_params=pltpu.CompilerParams(vmem_limit_bytes=56 * 2**20),
-    )(received, w, wi, twist)
+        compiler_params=pltpu.CompilerParams(
+            collective_id=0, has_side_effects=True, vmem_limit_bytes=56 * 2**20
+        ),
+    )(arriving, taps, gate, inner_in, vals, w, wi, twist)
 
 
 def per_device(arriving, input_gate, input_inner, values, conv_out, filters, bias):
@@ -192,20 +339,21 @@
     channels, tokens = values.shape[1:]
     own = channels // tiles
     f32, bf16 = jnp.float32, jnp.bfloat16
-    route = [((i + 1) % sections, i) for i in range(sections)]
-    grad = lax.ppermute(arriving[0], "pipe", route).astype(f32)
-    inner_in, vals = input_inner[0].astype(f32), values[0].astype(f32)
-    inner = (inner_in * vals).astype(bf16)
-    d_out = (grad * input_gate[0].astype(f32)).astype(bf16)
+
+    def split(array):
+        return array[0].reshape(tiles, own, tokens)
+
+    grad, q = exchange(
+        split(arriving), split(filters), split(input_gate), split(input_inner), split(values),
+        tiles, sections,
+    )
+    grad = grad.reshape(channels, tokens).astype(f32)
+    q = q.reshape(2, channels, tokens).astype(f32)
+    d_out = (grad * input_gate[0].astype(f32)).astype(bf16).astype(f32)
     d_gate = (grad * conv_out[0].astype(f32)).astype(bf16)
-    sent = jnp.stack([filters[0], inner, d_out]).reshape(3, tiles, own, tokens)
-    received = lax.all_to_all(sent, "ctx", split_axis=1, concat_axis=1, tiled=True)
-    result = local_call(received)
-    q = lax.all_to_all(result, "ctx", split_axis=1, concat_axis=1, tiled=True)
-    q = q.reshape(2, channels, tokens).astype(f32)
-    dz = q[0] + bias[0][:, None] * d_out.astype(f32)
-    inner_gradient = (dz * vals).astype(bf16)
-    d_values = (dz * inner_in).astype(bf16)
+    dz = q[0] + bias[0][:, None] * d_out
+    inner_gradient = (dz * values[0].astype(f32)).astype(bf16)
+    d_values = (dz * input_inner[0].astype(f32)).astype(bf16)
     return (d_gate[None], inner_gradient[None], d_values[None], q[1][None])
 
 

time: 180 us -> 127 us (0.71)
  blocking collectives: 130 us -> 0 us
  Pallas kernels: 35 us -> 119 us
  other arithmetic: 5.73 us -> 2.43 us
  local copies, waits for them, and re-layouts: 5.63 us -> 3.36 us
    all_to_all x2 -> x0, blocking collectives: 130 us -> none  [the longest x1 78 us: per_device(): lax.all_to_all(sent, 'ctx', split_axis=1, concat_axis=1, tiled=True)]
    pallas_call x1, Pallas kernels: 35 us -> 119 us  [exchange(): pl.pallas_call(functools.partial(kernel, n, sections, group), in_specs=[h...]
    convert_element_type x3 -> x1, other arithmetic: 5.4 us -> 2.43 us  [per_device(): d_values = (dz * input_inner[0].astype(f32)).astype(bf16)]
    all_to_all x1 -> x0, local copies, waits for them, and re-layouts: 1.99 us -> none  [per_device(): lax.all_to_all(sent, 'ctx', split_axis=1, concat_axis=1, tiled=True)]
    pallas_call x1 -> x0, local copies, waits for them, and re-layouts: 1.8 us -> none  [local_call(): pl.pallas_call(body, grid=(own // group,), in_specs=[pl.BlockSpec((3, til...]
  transfers between devices with their start and end apart: 1 -> 0, of which waited for: 1 -> 0; matrix products, arithmetic and copies ran while one was open for 1% -> 0% of each run, Pallas kernels for 0% -> 0%
where the time goes in v2:
time: 127 us; the launch traced here: 126 us
  Pallas kernels  119 us (94%)
  local copies, waits for them, and re-layouts  3.36 us (3%)
  other arithmetic  2.43 us (2%)
    pallas_call x1, Pallas kernels, exchange(): pl.pallas_call(functools.partial(kernel, n, sections, group), in_specs=[h...  119 us
    slice x1, local copies, waits for them, and re-layouts, per_device(): return (d_gate[None], inner_gradient[None], d_values[None], q[1][None])  3.32 us

profile of v2, /device:TPU:8, one launch (start us, length us, event | category | flops | bytes accessed | tf_op | source)
XLA Modules:
  0.0 125.8 jit_solution(12319299937460354859)
XLA Ops:
  0.6 119.3 %shard_map.132 = (bf16[16,256,128]{2,1,0:T(8,128)(2,1)}, bf16[2,16,256,128]{3,2,1,0:T(8,128)(2,1)}) custom-call(bf16[16,256,128]{2,1,0:T(8,128)(2,1)} %bitcast.27, bf16[16,256,128]{2,1,0:T(8,128)(2,1)} %bitcast.28, bf16[16,256,128]{2,1,0:T(8,128)(2,1)} %bitcast.23, bf16[16,256,128]{2,1,0:T(8,128)(2,1)} %bitcast.22, bf16[16,256,128]{2,1,0:T(8,128)(2,1)} %bitcast.24, ...), custom_call_target="tpu_custom_call" | custom-call | tf_op jit(solution)/shard_map/pallas_call | solution.py:312
  119.9 0.0 copy-start
  119.9 0.0 copy-start.1
  119.9 0.0 copy-start.2
  119.9 0.0 copy-start.3
  119.9 0.0 copy-start.4
  119.9 0.0 copy-start.5
  120.0 3.3 %fusion.2 = (f32[1,16,256,128]{3,2,1,0:T(8,128)}, f32[1,16,256,128]{3,2,1,0:T(8,128)S(1)}) fusion(bf16[2,16,256,128]{3,2,1,0:T(8,128)(2,1)} %get-tuple-element.7), kind=kLoop, calls=%fused_computation.7 | loop fusion | bytes 8388608 | tf_op jit(solution)/shard_map/slice | solution.py:357
  123.3 0.0 copy-done
  123.3 0.0 copy-done.1
  123.3 0.0 copy-done.2
  123.3 0.0 copy-done.3
  123.3 0.0 copy-done.4
  123.3 0.0 copy-done.5
  123.3 2.4 %multiply_convert_fusion = (bf16[1,4096,128]{2,1,0:T(8,128)(2,1)}, bf16[1,4096,128]{2,1,0:T(8,128)(2,1)}, bf16[1,4096,128]{2,1,0:T(8,128)(2,1)}) fusion(bf16[1,4096,128]{2,1,0:T(8,128)(2,1)S(1)} %copy-done, f32[1,16,256,128]{3,2,1,0:T(8,128)S(1)} %get-tuple-element.11, f32[4096]{0:T(1024)S(1)} %bitcast.29, bf16[1,4096,128]{2,1,0:T(8,128)(2,1)S(1)} %copy-done.1, ...), kind=kLoop, calls=%fused_computation.5 | loop fusion | flops 8388608 | bytes 10502144 | tf_op jit(solution)/shard_map/convert_element_type | solution.py:356
Async XLA Ops:
  119.9 3.4 %copy-start = (bf16[1,4096,128]{2,1,0:T(8,128)(2,1)S(1)}, bf16[1,4096,128]{2,1,0:T(8,128)(2,1)}, u32[]{:S(2)}) copy-start(bf16[1,4096,128]{2,1,0:T(8,128)(2,1)} %param.12) | copy-start | bytes 3145732
  119.9 3.4 %copy-start.1 = (bf16[1,4096,128]{2,1,0:T(8,128)(2,1)S(1)}, bf16[1,4096,128]{2,1,0:T(8,128)(2,1)}, u32[]{:S(2)}) copy-start(bf16[1,4096,128]{2,1,0:T(8,128)(2,1)} %param.11) | copy-start | bytes 3145732
  119.9 3.4 %copy-start.2 = (bf16[1,4096,128]{2,1,0:T(8,128)(2,1)S(1)}, bf16[1,4096,128]{2,1,0:T(8,128)(2,1)}, u32[]{:S(2)}) copy-start(bf16[1,4096,128]{2,1,0:T(8,128)(2,1)} %param.13) | copy-start | bytes 3145732
  119.9 3.4 %copy-start.3 = (bf16[1,4096,128]{2,1,0:T(8,128)(2,1)S(1)}, bf16[1,4096,128]{2,1,0:T(8,128)(2,1)}, u32[]{:S(2)}) copy-start(bf16[1,4096,128]{2,1,0:T(8,128)(2,1)} %param.14) | copy-start | bytes 3145732
  119.9 3.4 %copy-start.4 = (bf16[16,256,128]{2,1,0:T(8,128)(2,1)S(1)}, bf16[16,256,128]{2,1,0:T(8,128)(2,1)}, u32[]{:S(2)}) copy-start(bf16[16,256,128]{2,1,0:T(8,128)(2,1)} %get-tuple-element.6) | copy-start | bytes 3145732
  119.9 3.4 %copy-start.5 = (f32[1,4096]{1,0:T(1,128)S(1)}, f32[1,4096]{1,0:T(1,128)}, u32[]{:S(2)}) copy-start(f32[1,4096]{1,0:T(1,128)} %param.16) | copy-start | bytes 49156

commit v3 on v2

--- a/solution.py
+++ b/solution.py
@@ -3,7 +3,6 @@
 
 import jax
 import jax.numpy as jnp
-import numpy as np
 from jax import lax
 from jax.experimental import pallas as pl
 from jax.experimental.pallas import tpu as pltpu
@@ -71,23 +70,32 @@
     return [v for pair in zip(first, second) for v in pair]
 
 
-def tables(tiles, tokens):
-    full = 2 * tiles * tokens
-    j = np.arange(tokens)
-    phase = 2 * np.pi * ((j[:, None] * j[None, :]) % tokens) / tokens
-    cb, sb = np.cos(phase), np.sin(phase)
-    forward = np.block([[cb, -sb], [sb, cb]])
-    k = np.arange(tiles + 1)
-    angle = 2 * np.pi * ((k[:, None] * j[None, :]) % full) / full
-    twist = np.stack([np.cos(angle), np.sin(angle)], axis=1)
-    return (
-        jnp.asarray(forward, jnp.bfloat16),
-        jnp.asarray(forward.T, jnp.bfloat16),
-        jnp.asarray(twist, jnp.float32),
-    )
+def make_tables(w, wi, twist):
+    tokens = w.shape[0] // 2
+    tiles = twist.shape[0] - 1
+    j = lax.broadcasted_iota(jnp.int32, (tokens, tokens), 0)
+    k = lax.broadcasted_iota(jnp.int32, (tokens, tokens), 1)
+    phase = lax.rem(j * k, tokens).astype(jnp.float32) * (2.0 * math.pi / tokens)
+    cb, sb = jnp.cos(phase).astype(jnp.bfloat16), jnp.sin(phase).astype(jnp.bfloat16)
+    for ref, sign in ((w, -1.0), (wi, 1.0)):
+        ref[0:tokens, 0:tokens] = cb
+        ref[tokens : 2 * tokens, tokens : 2 * tokens] = cb
+        ref[0:tokens, tokens : 2 * tokens] = sb * sign
+        ref[tokens : 2 * tokens, 0:tokens] = sb * -sign
+    lane = lax.broadcasted_iota(jnp.int32, (1, tokens), 1)
+    unit = 2.0 * math.pi / (2 * tiles * tokens)
+
+    def row(t, carry):
+        angle = (lane * t).astype(jnp.float32) * unit
+        twist[t, 0:1, :] = jnp.cos(angle)
+        twist[t, 1:2, :] = jnp.sin(angle)
+        return carry
+
+    lax.fori_loop(0, tiles + 1, row, 0)
 
 
 ROWS = 16
+VMEM_MIB = 49
 
 
 def transform(rx, out, w, wi, twist, spec, back):
@@ -160,10 +168,11 @@
 
 def kernel(
     n, sections, group,
-    arriving, taps, gate, inner_in, vals, w, wi, twist,
-    grad_out, q,
-    grad, stage, rx, res, spec, back,
-    pair_send, pair_recv, send, recv, home, back_send, back_recv, back_home, grad_home,
+    arriving, taps, gate_in, inner_src, vals_src, saved_src, bias,
+    gate_out, inner_out, vals_out, taps_out,
+    gate, inner_in, vals, saved, w, wi, twist,
+    grad, stage, rx, res, q, biased, spec, back,
+    loads, pair_send, pair_recv, send, recv, home, back_send, back_recv, back_home,
 ):
     me, sec = lax.axis_index("ctx"), lax.axis_index("pipe")
     groups = arriving.shape[1] // group
@@ -174,6 +183,13 @@
     def peer_of(d):
         return lax.rem(me + d, n)
 
+    def load(i):
+        src = (inner_src, vals_src, gate_in, saved_src)[i]
+        dst = (inner_in, vals, gate, saved)[i]
+        return pltpu.make_async_copy(src, dst, loads.at[i])
+
+    for i in range(4):
+        load(i).start()
     barrier = pltpu.get_barrier_semaphore()
     pl.semaphore_signal(
         barrier, inc=1, device_id={"pipe": lax.rem(sec + 1, sections)}, device_id_type=MESH
@@ -215,11 +231,6 @@
     def own_taps(g):
         return pltpu.make_async_copy(taps.at[me, rows_of(g)], rx.at[g, 0, me], home.at[g])
 
-    def keep_grad(g):
-        return pltpu.make_async_copy(
-            grad.at[:, rows_of(g)], grad_out.at[:, rows_of(g)], grad_home.at[g]
-        )
-
     def forward(g, carry):
         rows = rows_of(g)
 
@@ -251,15 +262,40 @@
 
         product(inner_in, vals, 1)
         pair(g).wait_recv()
-        keep_grad(g).start()
         product(grad, gate, 2)
         return carry
 
+    for i in range(3):
+        load(i).wait()
     lax.fori_loop(0, groups, forward, 0)
+    load(3).wait()
+    make_tables(w, wi, twist)
+    own, tokens = arriving.shape[1:]
+    lanes = 128
+    f32 = jnp.float32
+
+    def side(b, carry):
+        if own >= lanes:
+            per = own // lanes
+            at = (lax.div(b, per), pl.ds(pl.multiple_of(lax.rem(b, per) * lanes, lanes), lanes))
+        else:
+            at = (pl.ds(b * (lanes // own), lanes // own),)
+        shape = grad[at].shape
+        g = grad[at].astype(f32).reshape(lanes, tokens)
+        gate_out[at] = (g * saved[at].astype(f32).reshape(lanes, tokens)).astype(
+            jnp.bfloat16
+        ).reshape(shape)
+        d_out = (g * gate[at].astype(f32).reshape(lanes, tokens)).astype(jnp.bfloat16)
+        row = bias[:, pl.ds(pl.multiple_of(b * lanes, lanes), lanes)]
+        column = jnp.transpose(jnp.broadcast_to(row, (tokens, lanes)))
+        biased[at] = (column * d_out.astype(f32)).reshape(shape)
+        return carry
+
+    lax.fori_loop(0, n * own // lanes, side, 0)
 
     def own_result(g):
         return pltpu.make_async_copy(
-            res.at[g, :, me], q.at[:, me, rows_of(g)], back_home.at[g]
+            res.at[g, :, me], q.at[g, :, me], back_home.at[g]
         )
 
     def turn_group(g, carry):
@@ -271,9 +307,9 @@
         def reply(d, c):
             pltpu.make_async_remote_copy(
                 src_ref=res.at[g, :, peer_of(d)],
-                dst_ref=q.at[:, me, rows_of(g)],
+                dst_ref=q.at[g, :, me],
                 send_sem=back_send.at[g],
-                recv_sem=back_recv.at[0],
+                recv_sem=back_recv.at[g],
                 device_id={"ctx": peer_of(d)},
                 device_id_type=MESH,
             ).start()
@@ -286,9 +322,20 @@
     lax.fori_loop(0, groups, turn_group, 0)
 
     def finish(g, carry):
+        rows = rows_of(g)
+        replies = q.at[g, :, pl.ds(0, n - 1)]
+        pltpu.make_async_copy(replies, replies, back_recv.at[g]).wait()
+        own_result(g).wait()
+
+        def product(p, c):
+            dz = q[g, 0, p].astype(f32) + biased[p, rows]
+            inner_out[p, rows] = (dz * vals[p, rows].astype(f32)).astype(jnp.bfloat16)
+            vals_out[p, rows] = (dz * inner_in[p, rows].astype(f32)).astype(jnp.bfloat16)
+            taps_out[p, rows] = q[g, 1, p]
+            return c
+
+        lax.fori_loop(0, n, product, 0)
         pair(g).wait_send()
-        keep_grad(g).wait()
-        own_result(g).wait()
         sent = rx.at[g, :, pl.ds(0, n - 1)]
         pltpu.make_async_copy(sent, sent, send.at[g]).wait()
         replied = res.at[g, :, pl.ds(0, n - 1)]
@@ -296,41 +343,87 @@
         return carry
 
     lax.fori_loop(0, groups, finish, 0)
-    everything = q.at[:, pl.ds(0, n - 1)]
-    pltpu.make_async_copy(everything, everything, back_recv.at[0]).wait()
-
-
-def exchange(arriving, taps, gate, inner_in, vals, n, sections):
+
+
+def exchange(arriving, taps, gate, inner_in, vals, saved, bias, n, sections):
     _, own, tokens = arriving.shape
     group = max(ROWS, own // 4)
     groups = own // group
-    w, wi, twist = tables(n, tokens)
     bf16 = jnp.bfloat16
     vmem = pl.BlockSpec(memory_space=pltpu.VMEM)
-    hbm = pl.BlockSpec(memory_space=pl.ANY)
+    hbm = pl.BlockSpec(memory_space=pltpu.HBM)
     dma = pltpu.SemaphoreType.DMA
+    whole = jax.ShapeDtypeStruct((n, own, tokens), bf16)
+    held = pltpu.VMEM((n, own, tokens), bf16)
     return pl.pallas_call(
         functools.partial(kernel, n, sections, group),
-        in_specs=[hbm, hbm, vmem, vmem, vmem, vmem, vmem, vmem],
-        out_specs=[hbm, hbm],
-        out_shape=[
-            jax.ShapeDtypeStruct((n, own, tokens), bf16),
-            jax.ShapeDtypeStruct((2, n, own, tokens), bf16),
-        ],
+        in_specs=[hbm] * 6 + [vmem],
+        out_specs=[vmem] * 4,
+        out_shape=[whole] * 4,
         scratch_shapes=[
-            pltpu.VMEM((n, own, tokens), bf16),
+            held, held, held, held,
+            pltpu.VMEM((2 * tokens, 2 * tokens), bf16),
+            pltpu.VMEM((2 * tokens, 2 * tokens), bf16),
+            pltpu.VMEM((n + 1, 2, tokens), jnp.float32),
+            held,
             pltpu.VMEM((groups, 2, n, group, tokens), bf16),
             pltpu.VMEM((groups, 3, n, group, tokens), bf16),
             pltpu.VMEM((groups, 2, n, group, tokens), bf16),
+            pltpu.VMEM((groups, 2, n, group, tokens), bf16),
+            pltpu.VMEM((n, own, tokens), jnp.float32),
             pltpu.VMEM((3, n + 1, group, 2 * tokens), bf16),
             pltpu.VMEM((2, n + 1, group, 2 * tokens), bf16),
+            dma((4,)),
             dma((groups,)), dma((groups,)), dma((groups,)), dma((groups,)), dma((groups,)),
-            dma((groups,)), dma((1,)), dma((groups,)), dma((groups,)),
+            dma((groups,)), dma((groups,)), dma((groups,)),
         ],
         compiler_params=pltpu.CompilerParams(
-            collective_id=0, has_side_effects=True, vmem_limit_bytes=56 * 2**20
+            collective_id=0, has_side_effects=True, vmem_limit_bytes=VMEM_MIB * 2**20
         ),
-    )(arriving, taps, gate, inner_in, vals, w, wi, twist)
+    )(arriving, taps, gate, inner_in, vals, saved, bias)
+
+
+def write_out(a, b, c, narrow, a_out, b_out, c_out, wide_out, wide, sems):
+    n = narrow.shape[0]
+    part = max(1, n // 4)
+    plain = [
+        pltpu.make_async_copy(src, dst, sems.at[i])
+        for i, (src, dst) in enumerate(((a, a_out), (b, b_out), (c, c_out)))
+    ]
+    for copy in plain:
+        copy.start()
+    widened = []
+    for i in range(n // part):
+
+        def widen(p, carry):
+            wide[p] = narrow[p].astype(jnp.float32)
+            return carry
+
+        lax.fori_loop(i * part, (i + 1) * part, widen, 0)
+        at = pl.ds(i * part, part)
+        copy = pltpu.make_async_copy(wide.at[at], wide_out.at[at], sems.at[3 + i])
+        copy.start()
+        widened.append(copy)
+    for copy in plain + widened:
+        copy.wait()
+
+
+def finish_outputs(d_gate, inner_gradient, d_values, d_filters):
+    shape = d_gate.shape
+    vmem = pl.BlockSpec(memory_space=pltpu.VMEM)
+    hbm = pl.BlockSpec(memory_space=pl.ANY)
+    narrow = jax.ShapeDtypeStruct(shape, jnp.bfloat16)
+    return pl.pallas_call(
+        write_out,
+        in_specs=[vmem] * 4,
+        out_specs=[hbm] * 4,
+        out_shape=[narrow] * 3 + [jax.ShapeDtypeStruct(shape, jnp.float32)],
+        scratch_shapes=[
+            pltpu.VMEM(shape, jnp.float32),
+            pltpu.SemaphoreType.DMA((3 + shape[0] // max(1, shape[0] // 4),)),
+        ],
+        compiler_params=pltpu.CompilerParams(vmem_limit_bytes=VMEM_MIB * 2**20),
+    )(d_gate, inner_gradient, d_values, d_filters)
 
 
 def per_device(arriving, input_gate, input_inner, values, conv_out, filters, bias):
@@ -338,23 +431,15 @@
     sections = lax.axis_size("pipe")
     channels, tokens = values.shape[1:]
     own = channels // tiles
-    f32, bf16 = jnp.float32, jnp.bfloat16
 
     def split(array):
         return array[0].reshape(tiles, own, tokens)
 
-    grad, q = exchange(
+    outs = exchange(
         split(arriving), split(filters), split(input_gate), split(input_inner), split(values),
-        tiles, sections,
+        split(conv_out), bias, tiles, sections,
     )
-    grad = grad.reshape(channels, tokens).astype(f32)
-    q = q.reshape(2, channels, tokens).astype(f32)
-    d_out = (grad * input_gate[0].astype(f32)).astype(bf16).astype(f32)
-    d_gate = (grad * conv_out[0].astype(f32)).astype(bf16)
-    dz = q[0] + bias[0][:, None] * d_out
-    inner_gradient = (dz * values[0].astype(f32)).astype(bf16)
-    d_values = (dz * input_inner[0].astype(f32)).astype(bf16)
-    return (d_gate[None], inner_gradient[None], d_values[None], q[1][None])
+    return tuple(array.reshape(1, channels, tokens) for array in finish_outputs(*outs))
 
 
 def solution(mesh):

time: 127 us -> 123 us (0.969)
  local copies, waits for them, and re-layouts: 3.36 us -> 0.71 us
  other arithmetic: 2.43 us -> 0 us
    slice x1 -> x0, local copies, waits for them, and re-layouts: 3.32 us -> none  [per_device(): return (d_gate[None], inner_gradient[None], d_values[None], q[1][None])]
    convert_element_type x1 -> x0, other arithmetic: 2.43 us -> none  [per_device(): d_values = (dz * input_inner[0].astype(f32)).astype(bf16)]
    pallas_call x0 -> x1, Pallas kernels: none -> 2.39 us  [finish_outputs(): pl.pallas_call(write_out, in_specs=[vmem] * 4, out_specs=[hbm] * 4, out_s...]
    pallas_call x1, Pallas kernels: 119 us -> 118 us  [exchange(): pl.pallas_call(functools.partial(kernel, n, sections, group), in_specs=[h...]
where the time goes in v3:
time: 123 us; the launch traced here: 122 us
  Pallas kernels  120 us (98%)
    pallas_call x1, Pallas kernels, exchange(): pl.pallas_call(functools.partial(kernel, n, sections, group), in_specs=[h...  118 us

profile of v3, /device:TPU:8, one launch (start us, length us, event | category | flops | bytes accessed | tf_op | source)
XLA Modules:
  0.0 121.6 jit_solution(8418338269588168408)
XLA Ops:
  0.6 0.0 copy-start
  0.6 0.7 copy-done
  1.4 117.8 %shard_map.102 = (bf16[16,256,128]{2,1,0:T(8,128)(2,1)S(1)}, bf16[16,256,128]{2,1,0:T(8,128)(2,1)S(1)}, bf16[16,256,128]{2,1,0:T(8,128)(2,1)S(1)}, bf16[16,256,128]{2,1,0:T(8,128)(2,1)S(1)}) custom-call(bf16[16,256,128]{2,1,0:T(8,128)(2,1)} %bitcast.10, bf16[16,256,128]{2,1,0:T(8,128)(2,1)} %bitcast.11, bf16[16,256,128]{2,1,0:T(8,128)(2,1)} %bitcast.12, ...), custom_call_target="tpu_custom_call" | custom-call | tf_op jit(solution)/shard_map/pallas_call | solution.py:358
  119.2 2.4 %shard_map.103 = (bf16[16,256,128]{2,1,0:T(8,128)(2,1)}, bf16[16,256,128]{2,1,0:T(8,128)(2,1)}, bf16[16,256,128]{2,1,0:T(8,128)(2,1)}, f32[16,256,128]{2,1,0:T(8,128)}) custom-call(bf16[16,256,128]{2,1,0:T(8,128)(2,1)S(1)} %get-tuple-element.12.a, bf16[16,256,128]{2,1,0:T(8,128)(2,1)S(1)} %get-tuple-element.13.b, ...), custom_call_target="tpu_custom_call" | custom-call | tf_op jit(solution)/shard_map/pallas_call | solution.py:416
Async XLA Ops:
  0.6 0.7 copy-start
